TPU v7x, 32 devices: a whole 2x2x4 slice. The times are simulated.
32 devices in a mesh: row: 8 (over y, x, core), col: 4 (over z).
Axes of the slice: x: 2, y: 2, z: 4, core: 2. Of those that a mesh axis runs over, the one named last changes fastest.
Arguments:
- features: bfloat16 [512, 256, 256], P('row', 'col'), may hold values from -6 to 6
- conv_expand: bfloat16 [256, 1024], replicated, may hold values from -0.375 to 0.375
- conv_kernel: bfloat16 [9, 1024], replicated, may hold values from -2 to 2
- conv_reduce: bfloat16 [1024, 256], replicated, may hold values from -0.1875 to 0.1875
- block_attend: bfloat16 [256, 768], replicated, as said below
- block_merge: bfloat16 [256, 256], replicated, may hold values from -0.375 to 0.375
- block_expand: bfloat16 [256, 1024], replicated, may hold values from -0.375 to 0.375
- block_reduce: bfloat16 [1024, 256], replicated, may hold values from -0.1875 to 0.1875
- grid_attend: bfloat16 [256, 768], replicated, as said below
- grid_merge: bfloat16 [256, 256], replicated, may hold values from -0.375 to 0.375
- grid_expand: bfloat16 [256, 1024], replicated, may hold values from -0.375 to 0.375
- grid_reduce: bfloat16 [1024, 256], replicated, may hold values from -0.1875 to 0.1875
- block_valid: int32 [64, 32], P('row', 'col'), may hold values from 0 to 1, as said below
- grid_valid: int32 [1, 64, 1, 32], P(None, 'row', None, 'col'), may hold values from 0 to 1, as said below
Outputs:
- output: bfloat16 [512, 256, 256], P('row', 'col')
Inputs may be any that keep to these rules, and one draw needn't show every extreme that they name: `block_valid`: 1 marks a window whose tokens go through the section, 0 one whose tokens pass unchanged. `grid_valid`: 1 marks a window whose tokens go through the section, 0 one whose tokens pass unchanged. `block_attend`: columns are queries, keys and values. `grid_attend`: columns are queries, keys and values.
All inputs are finite; a program needn't handle non-finite values.
Results may differ from a plain program's by a relative error of at most 0.01.
Values may be sent and summed in bfloat16 or wider, within the bound.
No kernel may reach another device: no remote copies, remote signals or barrier semaphores. Data moves between devices by JAX's collectives and lax.ppermute only.
A program may use at most 192 MiB of HBM per device.

v0:
```python
import jax
import jax.numpy as jnp
from jax import lax
from jax.sharding import PartitionSpec as P

HEADS = 8
WIN = 8
GRID = 8


EPSILON = 1e-05


def with_halo(array, sides, width):
    for axis, dim in sides:
        size, length = (lax.axis_size(axis), array.shape[dim])
        up = [(i, (i + 1) % size) for i in range(size - 1)]
        down = [(j, i) for i, j in up]
        last = lax.slice_in_dim(array, length - width, length, axis=dim)
        first = lax.slice_in_dim(array, 0, width, axis=dim)
        before = lax.ppermute(last, axis, up)
        after = lax.ppermute(first, axis, down)
        array = jnp.concatenate([before, array, after], axis=dim)
    return array


def layer_norm(values):
    widened = values.astype(jnp.float32)
    centred = widened - jnp.mean(widened, axis=-1, keepdims=True)
    variance = jnp.mean(centred * centred, axis=-1, keepdims=True)
    return (centred * lax.rsqrt(variance + EPSILON)).astype(jnp.bfloat16)


def attend_windows(windows, attend, merge):
    window_count, tokens_per, channels = windows.shape
    head_width = channels // HEADS
    normed = layer_norm(windows)
    packed = jnp.dot(
        normed.reshape(window_count * tokens_per, channels),
        attend,
        preferred_element_type=jnp.float32,
    ).astype(jnp.bfloat16)
    packed = packed.reshape(window_count, tokens_per, 3, HEADS, head_width)
    scores = jnp.einsum(
        "wqhd,wkhd->whqk", packed[:, :, 0], packed[:, :, 1], preferred_element_type=jnp.float32
    ) * head_width ** (-0.5)
    probs = jax.nn.softmax(scores, axis=-1).astype(jnp.bfloat16)
    mixed = jnp.einsum(
        "whqk,wkhd->wqhd", probs, packed[:, :, 2], preferred_element_type=jnp.float32
    ).astype(jnp.bfloat16)
    merged = jnp.dot(
        mixed.reshape(window_count * tokens_per, channels),
        merge,
        preferred_element_type=jnp.float32,
    )
    return merged.reshape(window_count, tokens_per, channels)


def window_section(windows, flags, attend, merge, expand, reduce_weight):
    window_count, tokens_per, channels = windows.shape
    alive_mask = flags.astype(jnp.float32)[:, None, None]
    attended = (
        windows.astype(jnp.float32) + alive_mask * attend_windows(windows, attend, merge)
    ).astype(jnp.bfloat16)
    normed = layer_norm(attended).reshape(window_count * tokens_per, channels)
    hidden = jax.nn.gelu(
        jnp.dot(normed, expand, preferred_element_type=jnp.float32), approximate=False
    ).astype(jnp.bfloat16)
    reduced = jnp.dot(hidden, reduce_weight, preferred_element_type=jnp.float32).reshape(
        window_count, tokens_per, channels
    )
    return (attended.astype(jnp.float32) + alive_mask * reduced).astype(jnp.bfloat16)


def mbconv(features, conv_expand, conv_kernel, conv_reduce):
    height, breadth, channels = features.shape
    normed = layer_norm(features)
    expanded = jax.nn.gelu(
        jnp.dot(
            normed.reshape(height * breadth, channels),
            conv_expand,
            preferred_element_type=jnp.float32,
        ),
        approximate=False,
    ).astype(jnp.bfloat16)
    padded = with_halo(expanded.reshape(height, breadth, -1), (("row", 0), ("col", 1)), 1)
    kernel_taps = conv_kernel.astype(jnp.float32)
    summed = jnp.zeros((height, breadth, padded.shape[-1]), jnp.float32)
    for position in range(9):
        shift_row = position // 3
        shift_col = position % 3
        summed = (
            summed
            + padded[shift_row : shift_row + height, shift_col : shift_col + breadth].astype(
                jnp.float32
            )
            * kernel_taps[position]
        )
    spatial = jax.nn.gelu(summed, approximate=False).astype(jnp.bfloat16)
    projected = jnp.dot(
        spatial.reshape(height * breadth, -1), conv_reduce, preferred_element_type=jnp.float32
    )
    return (features.astype(jnp.float32) + projected.reshape(height, breadth, channels)).astype(
        jnp.bfloat16
    )


def grid_shape(height, breadth):
    rows_count = lax.axis_size("row")
    cols_count = lax.axis_size("col")
    repeat_rows = max(1, GRID // rows_count)
    repeat_cols = max(1, GRID // cols_count)
    step_rows = height // (repeat_rows * rows_count)
    step_cols = breadth // (repeat_cols * cols_count)
    parity_rows = max(1, rows_count // GRID)
    parity_cols = max(1, cols_count // GRID)
    return (
        rows_count,
        cols_count,
        repeat_rows,
        repeat_cols,
        step_rows,
        step_cols,
        parity_rows,
        parity_cols,
    )


def to_grid(tokens):
    height, breadth, channels = tokens.shape
    (
        rows_count,
        cols_count,
        repeat_rows,
        repeat_cols,
        step_rows,
        step_cols,
        parity_rows,
        parity_cols,
    ) = grid_shape(height, breadth)
    divided = tokens.reshape(
        repeat_rows, rows_count, step_rows, repeat_cols, cols_count, step_cols, channels
    )
    flattened = jnp.transpose(divided, (1, 4, 0, 2, 3, 5, 6)).reshape(
        rows_count * cols_count, repeat_rows, step_rows, repeat_cols, step_cols, channels
    )
    arrived = lax.all_to_all(flattened, ("row", "col"), split_axis=0, concat_axis=0, tiled=True)
    ordered = arrived.reshape(
        rows_count // parity_rows,
        parity_rows,
        cols_count // parity_cols,
        parity_cols,
        repeat_rows,
        step_rows,
        repeat_cols,
        step_cols,
        channels,
    )
    windows = jnp.transpose(ordered, (1, 5, 3, 7, 0, 4, 2, 6, 8))
    return windows.reshape(-1, GRID * GRID, channels)


def from_grid(windows, height, breadth):
    channels = windows.shape[-1]
    (
        rows_count,
        cols_count,
        repeat_rows,
        repeat_cols,
        step_rows,
        step_cols,
        parity_rows,
        parity_cols,
    ) = grid_shape(height, breadth)
    ordered = windows.reshape(
        parity_rows,
        step_rows,
        parity_cols,
        step_cols,
        rows_count // parity_rows,
        repeat_rows,
        cols_count // parity_cols,
        repeat_cols,
        channels,
    )
    returning = jnp.transpose(ordered, (4, 0, 6, 2, 5, 1, 7, 3, 8)).reshape(
        rows_count * cols_count, repeat_rows, step_rows, repeat_cols, step_cols, channels
    )
    arrived = lax.all_to_all(returning, ("row", "col"), split_axis=0, concat_axis=0, tiled=True)
    divided = jnp.transpose(
        arrived.reshape(
            rows_count, cols_count, repeat_rows, step_rows, repeat_cols, step_cols, channels
        ),
        (2, 0, 3, 4, 1, 5, 6),
    )
    return divided.reshape(height, breadth, channels)


def on_device(
    features,
    conv_expand,
    conv_kernel,
    conv_reduce,
    block_attend,
    block_merge,
    block_expand,
    block_reduce,
    grid_attend,
    grid_merge,
    grid_expand,
    grid_reduce,
    block_valid,
    grid_valid,
):
    height, breadth, channels = features.shape
    after_conv = mbconv(features, conv_expand, conv_kernel, conv_reduce)
    blocks = (
        after_conv.reshape(height // WIN, WIN, breadth // WIN, WIN, channels)
        .transpose(0, 2, 1, 3, 4)
        .reshape(-1, WIN * WIN, channels)
    )
    sectioned = window_section(
        blocks, block_valid.reshape(-1), block_attend, block_merge, block_expand, block_reduce
    )
    after_block = (
        sectioned.reshape(height // WIN, breadth // WIN, WIN, WIN, channels)
        .transpose(0, 2, 1, 3, 4)
        .reshape(height, breadth, channels)
    )
    grids = to_grid(after_block)
    finished = window_section(
        grids, grid_valid.reshape(-1), grid_attend, grid_merge, grid_expand, grid_reduce
    )
    return from_grid(finished, height, breadth)


def solution(mesh):
    in_specs = (
        P("row", "col", None),
        P(),
        P(),
        P(),
        P(),
        P(),
        P(),
        P(),
        P(),
        P(),
        P(),
        P(),
        P("row", "col"),
        P(None, "row", None, "col"),
    )
    out_specs = P("row", "col", None)
    return jax.shard_map(
        on_device, mesh=mesh, in_specs=in_specs, out_specs=out_specs, check_vma=False
    )
```

profile of v0, /device:TPU:1, one launch (start us, length us, event | category | flops | bytes accessed | tf_op | source)
XLA Modules:
  0.0 612.9 jit_solution(11330713896446635716)
XLA Ops:
  7.4 38.6 %fusion.4 = bf16[4096,1024]{1,0:T(8,128)(2,1)S(1)} fusion(bf16[4096,256]{1,0:T(8,128)(2,1)S(1)} %bitcast.151, bf16[256,1024]{1,0:T(8,128)(2,1)S(1)} %copy-done), kind=kOutput, calls=%fused_computation.8 | convolution fusion | flops 2420113408 | bytes 11010048 | tf_op jit(solution)/shard_map/dot_general | solution.py:79
  49.2 4.5 collective-permute-start
  56.3 3.7 collective-permute-done.1
  69.3 4.1 collective-permute-done.3
  73.4 13.5 %maximum_maximum_fusion = (bf16[66,65,1024]{2,1,0:T(8,128)(2,1)S(1)}, bf16[66,65,1024]{2,1,0:T(8,128)(2,1)S(1)}) fusion(bf16[1,64,1024]{2,1,0:T(8,128)(2,1)S(1)} %collective-permute-done.1, bf16[64,64,1024]{2,1,0:T(8,128)(2,1)} %bitcast.132, bf16[1,64,1024]{2,1,0:T(8,128)(2,1)S(1)} %collective-permute-done, ...), kind=kLoop, calls=%fused_computation.87 | loop fusion | flops 70287360 | bytes 26492928 | tf_op jit(solution)/shard_map/concatenate | solution.py:23
  87.0 73.0 %fusion.74 = bf16[64,64,256]{2,1,0:T(8,128)(2,1)S(1)} fusion(bf16[64,64,256]{2,1,0:T(8,128)(2,1)S(1)} %copy-done.3, bf16[64,64,1024]{2,1,0:T(8,128)(2,1)S(1)} %bitcast.135, bf16[66,65,1024]{2,1,0:T(8,128)(2,1)S(1)} %get-tuple-element.12, bf16[1,64,1024]{2,1,0:T(8,128)(2,1)S(1)} %collective-permute-done.1, bf16[66,65,1024]{2,1,0:T(8,128)(2,1)S(1)} %get-tuple-element.11, ...), kind=kOutput, calls=%fused_computation.123 | convolution fusion | flops 2540699648 | bytes 63737856 | tf_op jit(solution)/shard_map/dot_general | solution.py:100
  167.9 4.5 convolution_convert_fusion.1
  172.4 8.6 %copy.60 = bf16[4096,768]{0,1:T(8,128)(2,1)} copy(bf16[4096,768]{1,0:T(8,128)(2,1)} %convolution_convert_fusion.1) | data formatting | bytes 12582912 | tf_op jit(solution)/shard_map/convert_element_type | solution.py:42
  181.0 17.9 %reshape.221 = bf16[64,64,3,8,32]{1,0,4,3,2:T(8,128)(2,1)} reshape(bf16[4096,768]{0,1:T(8,128)(2,1)} %copy.60) | data formatting | bytes 12582912 | tf_op jit(solution)/shard_map/reshape | solution.py:43
  198.9 7.5 %fusion.187 = (bf16[64,64,1,8,32]{1,0,4,3,2:T(8,128)(2,1)}, bf16[64,64,1,8,32]{1,0,4,3,2:T(8,128)(2,1)S(1)}, bf16[64,64,1,8,32]{1,0,4,3,2:T(8,128)(2,1)S(1)}) fusion(bf16[64,64,3,8,32]{1,0,4,3,2:T(8,128)(2,1)} %reshape.221), kind=kLoop, calls=%fused_computation.264 | loop fusion | bytes 12582912 | tf_op jit(solution)/shard_map/slice | solution.py:49
  206.4 21.2 %fusion.78 = f32[64,8,64,64]{2,3,1,0:T(8,128)} fusion(bf16[64,64,1,8,32]{1,0,4,3,2:T(8,128)(2,1)S(1)} %get-tuple-element.10, bf16[64,64,1,8,32]{1,0,4,3,2:T(8,128)(2,1)S(1)} %get-tuple-element.9), kind=kOutput, calls=%fused_computation.131 | convolution fusion | flops 134217728 | bytes 12582912 | tf_op jit(solution)/shard_map/wqhd,wkhd->whqk/dot_general | solution.py:44
  227.6 18.8 %fusion.189 = (f32[64,8,64]{2,1,0:T(8,128)S(1)}, f32[64,8,64,64]{2,3,1,0:T(8,128)}) fusion(f32[64,8,64,64]{2,3,1,0:T(8,128)} %fusion.78), kind=kOutput, calls=%fused_computation.266 | output fusion | flops 8388671 | bytes 16908288 | tf_op jit(solution)/shard_map/sub | solution.py:47
  246.4 18.0 %fusion.84 = bf16[64,8,32,64]{3,2,1,0:T(8,128)(2,1)} fusion(f32[64,8,64,64]{2,3,1,0:T(8,128)} %get-tuple-element.27, f32[64,8,64]{2,1,0:T(8,128)S(1)} %get-tuple-element.26, bf16[64,64,1,8,32]{1,0,4,3,2:T(8,128)(2,1)} %get-tuple-element.8), kind=kOutput, calls=%fused_computation.147 | convolution fusion | flops 139460608 | bytes 12713984 | tf_op jit(solution)/shard_map/whqk,wkhd->wqhd/dot_general | solution.py:48
  264.5 5.4 convert_reduce_fusion.1
  273.4 41.1 %fusion.54 = f32[4096,256]{1,0:T(8,128)} fusion(bf16[1024,256]{1,0:T(8,128)(2,1)S(1)} %copy-done.13, bf16[4096,256]{1,0:T(8,128)(2,1)} %bitcast.152, bf16[256,1024]{1,0:T(8,128)(2,1)} %param.20), kind=kOutput, calls=%fused_computation.96 | convolution fusion | flops 4567597056 | bytes 7340032 | tf_op jit(solution)/shard_map/dot_general | solution.py:69
  319.1 6.6 %all-to-all-start = ((bf16[32,1,8,2,8,256]{5,4,3,2,1,0:T(8,128)(2,1)}), bf16[32,1,8,2,8,256]{5,4,3,2,1,0:T(8,128)(2,1)S(1)}, u32[]{:S(2)}, u32[]{:S(2)}) async-start(bf16[32,1,8,2,8,256]{5,4,3,2,1,0:T(8,128)(2,1)} %bitcast.141), calls=%async_computation | async-start | bytes 4194304 | tf_op jit(solution)/shard_map/all_to_all | solution.py:147
  325.9 48.1 %all-to-all-done = bf16[32,1,8,2,8,256]{5,4,3,2,1,0:T(8,128)(2,1)S(1)} async-done(((bf16[32,1,8,2,8,256]{5,4,3,2,1,0:T(8,128)(2,1)}), bf16[32,1,8,2,8,256]{5,4,3,2,1,0:T(8,128)(2,1)S(1)}, u32[]{:S(2)}, u32[]{:S(2)}) %all-to-all-start) | async-done | bytes 2097184 | tf_op jit(solution)/shard_map/all_to_all | solution.py:147
  374.6 4.3 copy.111
  382.5 5.0 multiply_reduce_fusion.2
  388.5 6.1 reshape.236
  394.5 6.1 reshape.235
  401.9 5.9 convolution_convert_fusion
  407.8 8.6 %copy.70 = bf16[4096,768]{0,1:T(8,128)(2,1)} copy(bf16[4096,768]{1,0:T(8,128)(2,1)} %convolution_convert_fusion) | data formatting | bytes 12582912 | tf_op jit(solution)/shard_map/convert_element_type | solution.py:42
  416.4 18.0 %reshape.226 = bf16[64,64,3,8,32]{1,0,4,3,2:T(8,128)(2,1)} reshape(bf16[4096,768]{0,1:T(8,128)(2,1)} %copy.70) | data formatting | bytes 12582912 | tf_op jit(solution)/shard_map/reshape | solution.py:43
  434.5 7.5 %fusion.186 = (bf16[64,64,1,8,32]{1,0,4,3,2:T(8,128)(2,1)}, bf16[64,64,1,8,32]{1,0,4,3,2:T(8,128)(2,1)S(1)}, bf16[64,64,1,8,32]{1,0,4,3,2:T(8,128)(2,1)S(1)}) fusion(bf16[64,64,3,8,32]{1,0,4,3,2:T(8,128)(2,1)} %reshape.226), kind=kLoop, calls=%fused_computation.263 | loop fusion | bytes 12582912 | tf_op jit(solution)/shard_map/slice | solution.py:49
  442.0 21.2 %fusion.77 = f32[64,8,64,64]{2,3,1,0:T(8,128)} fusion(bf16[64,64,1,8,32]{1,0,4,3,2:T(8,128)(2,1)S(1)} %get-tuple-element.7, bf16[64,64,1,8,32]{1,0,4,3,2:T(8,128)(2,1)S(1)} %get-tuple-element.6), kind=kOutput, calls=%fused_computation.127 | convolution fusion | flops 134217728 | bytes 12582912 | tf_op jit(solution)/shard_map/wqhd,wkhd->whqk/dot_general | solution.py:44
  463.2 18.8 %fusion.190 = (f32[64,8,64]{2,1,0:T(8,128)S(1)}, f32[64,8,64,64]{2,3,1,0:T(8,128)}) fusion(f32[64,8,64,64]{2,3,1,0:T(8,128)} %fusion.77), kind=kOutput, calls=%fused_computation.267 | output fusion | flops 8388671 | bytes 16908288 | tf_op jit(solution)/shard_map/sub | solution.py:47
  482.0 18.0 %fusion.83 = bf16[64,8,32,64]{3,2,1,0:T(8,128)(2,1)} fusion(f32[64,8,64,64]{2,3,1,0:T(8,128)} %get-tuple-element.31, f32[64,8,64]{2,1,0:T(8,128)S(1)} %get-tuple-element.30, bf16[64,64,1,8,32]{1,0,4,3,2:T(8,128)(2,1)} %get-tuple-element.5), kind=kOutput, calls=%fused_computation.146 | convolution fusion | flops 139460608 | bytes 12713984 | tf_op jit(solution)/shard_map/whqk,wkhd->wqhd/dot_general | solution.py:48
  500.1 5.4 convert_reduce_fusion
  509.0 40.9 %fusion.52 = f32[4096,256]{1,0:T(8,128)} fusion(bf16[1024,256]{1,0:T(8,128)(2,1)S(1)} %copy-done.14, bf16[4096,256]{1,0:T(8,128)(2,1)} %bitcast.153, bf16[256,1024]{1,0:T(8,128)(2,1)} %param.24), kind=kOutput, calls=%fused_computation.95 | convolution fusion | flops 4567597056 | bytes 7340032 | tf_op jit(solution)/shard_map/dot_general | solution.py:69
  549.9 4.0 fusion.76
  559.0 52.1 %all_to_all.10 = bf16[32,1,8,2,8,256]{5,4,3,2,1,0:T(8,128)(2,1)S(1)} all-to-all(bf16[32,1,8,2,8,256]{5,4,3,2,1,0:T(8,128)(2,1)S(1)} %bitcast.144), channel_id=1, replica_groups=mesh['row'=8,'col'=4] {'row','col'}, dimensions={0} | all-to-all | bytes 4194304 | tf_op jit(solution)/shard_map/all_to_all | solution.py:189
  (80 shorter events, 54.8 us)
Async XLA Ops:
  0.0 7.3 %copy-start = (bf16[256,1024]{1,0:T(8,128)(2,1)S(1)}, bf16[256,1024]{1,0:T(8,128)(2,1)}, u32[]{:S(2)}) copy-start(bf16[256,1024]{1,0:T(8,128)(2,1)} %param.15) | copy-start | bytes 1572868
  7.3 48.3 %copy-start.10 = (s32[8,8]{1,0:T(8,128)S(1)}, s32[8,8]{1,0:T(8,128)}, u32[]{:S(2)}) copy-start(s32[8,8]{1,0:T(8,128)} %param.26) | copy-start | bytes 772
  7.4 59.5 %copy-start.8 = (bf16[9,1024]{1,0:T(8,128)(2,1)S(1)}, bf16[9,1024]{1,0:T(8,128)(2,1)}, u32[]{:S(2)}) copy-start(bf16[9,1024]{1,0:T(8,128)(2,1)} %param.16) | copy-start | bytes 55300
  46.0 3.2 copy-start.2
  49.2 7.1 %collective-permute-start = (bf16[1,64,1024]{2,1,0:T(8,128)(2,1)S(1)}, bf16[1,64,1024]{2,1,0:T(8,128)(2,1)S(1)}, u32[]{:S(2)}, u32[]{:S(2)}) collective-permute-start(bf16[1,64,1024]{2,1,0:T(8,128)(2,1)S(1)} %get-tuple-element.15), channel_id=1, source_target_pairs={{0,4},{4,8},{8,12},{12,16},{16,20},{20,24},{24,28},{1,5},{5,9},{9,... | collective-permute-start | bytes 393224 | tf_op jit(solution)/shard_map/ppermute | solution.py:21
  53.8 6.3 %collective-permute-start.1 = (bf16[1,64,1024]{2,1,0:T(8,128)(2,1)S(1)}, bf16[1,64,1024]{2,1,0:T(8,128)(2,1)S(1)}, u32[]{:S(2)}, u32[]{:S(2)}) collective-permute-start(bf16[1,64,1024]{2,1,0:T(8,128)(2,1)S(1)} %get-tuple-element.16), channel_id=1, source_target_pairs={{4,0},{8,4},{12,8},{16,12},{20,16},{24,20},{28,24},{5,1},{9,5},{13... | collective-permute-start | bytes 393224 | tf_op jit(solution)/shard_map/ppermute | solution.py:22
  60.0 26.9 %slice-start = ((s8[8388608]{0:T(1024)(128)(4,1)}), s8[4194304]{0:T(1024)(128)(4,1)S(1)}, s32[]{:S(2)}) async-start(s8[8388608]{0:T(1024)(128)(4,1)} %bitcast.133), calls=%async_computation.2 | async-start | bytes 8388608
  60.1 26.9 %copy-start.3 = (bf16[64,64,256]{2,1,0:T(8,128)(2,1)S(1)}, bf16[64,64,256]{2,1,0:T(8,128)(2,1)}, u32[]{:S(2)}) copy-start(bf16[64,64,256]{2,1,0:T(8,128)(2,1)} %param.14) | copy-start | bytes 6291460
  60.1 26.9 %copy-start.12 = (bf16[1024,256]{1,0:T(8,128)(2,1)S(1)}, bf16[1024,256]{1,0:T(8,128)(2,1)}, u32[]{:S(2)}) copy-start(bf16[1024,256]{1,0:T(8,128)(2,1)} %param.17) | copy-start | bytes 1572868
  62.2 7.1 %collective-permute-start.2 = (bf16[66,1,1024]{2,1,0:T(2,128)(2,1)S(1)}, bf16[66,1,1024]{2,1,0:T(2,128)(2,1)S(1)}, u32[]{:S(2)}, u32[]{:S(2)}) collective-permute-start(bf16[66,1,1024]{2,1,0:T(2,128)(2,1)S(1)} %get-tuple-element.13), channel_id=1, source_target_pairs={{0,1},{1,2},{2,3},{4,5},{5,6},{6,7},{8,9},{9,10},{10,11},{12,13},{... | collective-permute-start | bytes 405512 | tf_op jit(solution)/shard_map/ppermute | solution.py:21
  65.6 7.8 %collective-permute-start.3 = (bf16[66,1,1024]{2,1,0:T(2,128)(2,1)S(1)}, bf16[66,1,1024]{2,1,0:T(2,128)(2,1)S(1)}, u32[]{:S(2)}, u32[]{:S(2)}) collective-permute-start(bf16[66,1,1024]{2,1,0:T(2,128)(2,1)S(1)} %get-tuple-element.14), channel_id=1, source_target_pairs={{1,0},{2,1},{3,2},{5,4},{6,5},{7,6},{9,8},{10,9},{11,10},{13,12},{... | collective-permute-start | bytes 405512 | tf_op jit(solution)/shard_map/ppermute | solution.py:22
  66.9 20.0 %slice-start.1 = ((s8[8388608]{0:T(1024)(128)(4,1)}), s8[4194304]{0:T(1024)(128)(4,1)S(1)}, s32[]{:S(2)}) async-start(s8[8388608]{0:T(1024)(128)(4,1)} %bitcast.133), calls=%async_computation.3 | async-start | bytes 8388608
  160.1 7.8 %copy-start.5 = (bf16[256,768]{1,0:T(8,128)(2,1)S(1)}, bf16[256,768]{1,0:T(8,128)(2,1)}, u32[]{:S(2)}) copy-start(bf16[256,768]{1,0:T(8,128)(2,1)} %param.18) | copy-start | bytes 1179652
  246.4 18.1 %copy-start.6 = (bf16[256,256]{1,0:T(8,128)(2,1)S(1)}, bf16[256,256]{1,0:T(8,128)(2,1)}, u32[]{:S(2)}) copy-start(bf16[256,256]{1,0:T(8,128)(2,1)} %param.19) | copy-start | bytes 393220
  246.4 18.1 %copy-start.9 = (f32[64]{0:T(128)S(1)}, f32[64]{0:T(128)}, u32[]{:S(2)}) copy-start(f32[64]{0:T(128)} %convert_element_type.204) | copy-start | bytes 772
  264.5 9.0 %copy-start.13 = (bf16[1024,256]{1,0:T(8,128)(2,1)S(1)}, bf16[1024,256]{1,0:T(8,128)(2,1)}, u32[]{:S(2)}) copy-start(bf16[1024,256]{1,0:T(8,128)(2,1)} %param.21) | copy-start | bytes 1572868
  314.5 11.2 %copy-start.11 = (s32[1,8,1,8]{3,2,1,0:T(1,128)S(1)}, s32[1,8,1,8]{3,2,1,0:T(1,128)}, u32[]{:S(2)}) copy-start(s32[1,8,1,8]{3,2,1,0:T(1,128)} %param.27) | copy-start | bytes 772
  319.1 54.9 %all-to-all-start = ((bf16[32,1,8,2,8,256]{5,4,3,2,1,0:T(8,128)(2,1)}), bf16[32,1,8,2,8,256]{5,4,3,2,1,0:T(8,128)(2,1)S(1)}, u32[]{:S(2)}, u32[]{:S(2)}) async-start(bf16[32,1,8,2,8,256]{5,4,3,2,1,0:T(8,128)(2,1)} %bitcast.141), calls=%async_computation | async-start | bytes 4194304 | tf_op jit(solution)/shard_map/all_to_all | solution.py:147
  378.9 23.0 %copy-start.4 = (bf16[256,768]{1,0:T(8,128)(2,1)S(1)}, bf16[256,768]{1,0:T(8,128)(2,1)}, u32[]{:S(2)}) copy-start(bf16[256,768]{1,0:T(8,128)(2,1)} %param.22) | copy-start | bytes 1179652
  482.0 18.1 %copy-start.7 = (bf16[256,256]{1,0:T(8,128)(2,1)S(1)}, bf16[256,256]{1,0:T(8,128)(2,1)}, u32[]{:S(2)}) copy-start(bf16[256,256]{1,0:T(8,128)(2,1)} %param.23) | copy-start | bytes 393220
  500.0 9.0 %copy-start.14 = (bf16[1024,256]{1,0:T(8,128)(2,1)S(1)}, bf16[1024,256]{1,0:T(8,128)(2,1)}, u32[]{:S(2)}) copy-start(bf16[1024,256]{1,0:T(8,128)(2,1)} %param.25) | copy-start | bytes 1572868
  509.0 103.6 %copy-start.1 = (bf16[256,1024]{1,0:T(8,128)(2,1)S(1)}, bf16[256,1024]{1,0:T(8,128)(2,1)}, u32[]{:S(2)}) copy-start(bf16[256,1024]{1,0:T(8,128)(2,1)} %param.15) | copy-start | bytes 1572868
where the time goes:
time: 614 us; the launch traced here: 613 us
  matrix products  293 us (48%)
  local copies, waits for them, and re-layouts  102 us (17%)
  other arithmetic  88.9 us (14%)
  waiting for transfers between devices  58.3 us (9%)
  blocking collectives  52.1 us (8%)
  starting transfers between devices  17.7 us (3%)
    dot_general x2, matrix products, window_section(): jnp.dot(hidden, reduce_weight, preferred_element_type=jnp.float32)  82 us
    dot_general x1, matrix products, mbconv(): jnp.dot(spatial.reshape(height * breadth, -1), conv_reduce, preferred_ele...  73 us
    all_to_all x1, blocking collectives, from_grid(): lax.all_to_all(returning, ('row', 'col'), split_axis=0, concat_axis=0, ti...  52.1 us
    all_to_all x1, waiting for transfers between devices, to_grid(): lax.all_to_all(flattened, ('row', 'col'), split_axis=0, concat_axis=0, ti...  48.1 us
    dot_general x2, matrix products, attend_windows(): jnp.einsum('wqhd,wkhd->whqk', packed[:, :, 0], packed[:, :, 1], preferred...  42.4 us
    dot_general x1, matrix products, mbconv(): jnp.dot(normed.reshape(height * breadth, channels), conv_expand, preferre...  38.6 us
    sub x2, other arithmetic, attend_windows(): probs = jax.nn.softmax(scores, axis=-1).astype(jnp.bfloat16)  37.6 us
    dot_general x2, matrix products, attend_windows(): jnp.einsum('whqk,wkhd->wqhd', probs, packed[:, :, 2], preferred_element_t...  36.1 us
  transfers between devices with their start and end apart: 5, of which 4 were waited for; matrix products, arithmetic and copies ran while one was open for 0% of the time, Pallas kernels for 0%

commit v1 on v0

v1 whole, which is shorter than its diff:
```python
import functools

import jax
import jax.numpy as jnp
from jax import lax
from jax.experimental import pallas as pl
from jax.experimental.pallas import tpu as pltpu
from jax.sharding import PartitionSpec as P

HEADS = 8
WIN = 8
GRID = 8
EPSILON = 1e-05
LANES = 128
F32 = jnp.float32
BF16 = jnp.bfloat16


def dot(a, b):
    return jnp.dot(a, b, preferred_element_type=F32)


def dot_nt(a, b):
    return lax.dot_general(a, b, (((1,), (1,)), ((), ())), preferred_element_type=F32)


def gelu(x):
    return 0.5 * x * (1.0 + lax.erf(x * 0.7071067811865476))


def layer_norm(x):
    centred = x - jnp.mean(x, axis=-1, keepdims=True)
    variance = jnp.mean(centred * centred, axis=-1, keepdims=True)
    return (centred * lax.rsqrt(variance + EPSILON)).astype(BF16)


def section(x, flag_of, attend, merge, expand, reduce_weight):
    tokens, channels = x.shape
    per = WIN * WIN
    count = tokens // per
    head_width = channels // HEADS
    per_group = LANES // head_width
    groups = channels // LANES
    scale = head_width ** (-0.5) * 1.4426950408889634
    packed = dot(layer_norm(x), attend[...]).astype(BF16)
    lane = lax.broadcasted_iota(jnp.int32, (1, LANES), 1)
    masks = [jnp.where(lane // head_width == h, 1.0, 0.0).astype(BF16) for h in range(per_group)]
    low = lane < per
    row = lax.broadcasted_iota(jnp.int32, (per_group * per, LANES), 0)
    col = lax.broadcasted_iota(jnp.int32, (per_group * per, LANES), 1)
    ones = jnp.where(row // per == col // head_width, 1.0, 0.0).astype(BF16)
    mixed = []
    for g in range(groups):
        weights, tops = [], []
        for w in range(count):
            rows = slice(w * per, (w + 1) * per)
            q = packed[rows, g * LANES : (g + 1) * LANES]
            k = packed[rows, channels + g * LANES : channels + (g + 1) * LANES]
            v = packed[rows, 2 * channels + g * LANES : 2 * channels + (g + 1) * LANES]
            ks = jnp.concatenate([k * m for m in masks], axis=0)
            vs = jnp.concatenate([v * m for m in masks], axis=0)
            s = dot_nt(q, ks)
            parts = []
            for p in range(per_group * per // LANES):
                sp = s[:, p * LANES : (p + 1) * LANES]
                m0 = jnp.max(jnp.where(low, sp, -jnp.inf), axis=-1, keepdims=True)
                m1 = jnp.max(jnp.where(low, -jnp.inf, sp), axis=-1, keepdims=True)
                parts.append(jnp.exp2((sp - jnp.where(low, m0, m1)) * scale).astype(BF16))
            e = jnp.concatenate(parts, axis=1)
            weights.append(e)
            tops.append(dot(e, vs))
        total = dot(jnp.concatenate(weights, axis=0), ones)
        mixed.append((jnp.concatenate(tops, axis=0) / total).astype(BF16))
    merged = dot(jnp.concatenate(mixed, axis=1), merge[...])
    flags = [flag_of(w) for w in range(count)]

    def gated(base, update):
        return jnp.concatenate(
            [
                base[w * per : (w + 1) * per] + flags[w] * update[w * per : (w + 1) * per]
                for w in range(count)
            ],
            axis=0,
        )

    attended = gated(x, merged)
    normed = layer_norm(attended)
    hidden_width = expand.shape[1]
    step = min(256, hidden_width)
    reduced = None
    for start in range(0, hidden_width, step):
        hidden = gelu(dot(normed, expand[:, start : start + step])).astype(BF16)
        part = dot(hidden, reduce_weight[start : start + step, :])
        reduced = part if reduced is None else reduced + part
    return gated(attended, reduced)


def band_kernel(
    col_count,
    flags_ref,
    main_ref,
    above_ref,
    below_ref,
    top_ref,
    bottom_ref,
    sides_ref,
    conv_expand,
    conv_kernel,
    conv_reduce,
    attend,
    merge,
    expand,
    reduce_weight,
    out_ref,
):
    u = pl.program_id(0)
    last = pl.num_programs(0) - 1
    breadth, channels = main_ref.shape[1:]
    rows = WIN
    main = main_ref[...].astype(F32)
    above = jnp.where(u == 0, top_ref[...].astype(F32), above_ref[...].astype(F32))
    below = jnp.where(u == last, bottom_ref[...].astype(F32), below_ref[...].astype(F32))
    inner = (rows + 2) * breadth
    x = jnp.concatenate([above, main, below], axis=0).reshape(inner, channels)
    normed = layer_norm(jnp.concatenate([x, sides_ref[0].astype(F32)], axis=0))
    width = conv_expand.shape[1]
    step = min(256, width)
    column = lax.broadcasted_iota(jnp.int32, (1, breadth, 1), 1)
    first_col = column == 0
    last_col = column == breadth - 1
    taps = conv_kernel[...].astype(F32)
    projected = None
    for start in range(0, width, step):
        e = gelu(dot(normed, conv_expand[:, start : start + step]))
        body = e[:inner].reshape(rows + 2, breadth, step)
        side = e[inner:]
        sums, edges = [], []
        for j in range(3):
            k = [taps[3 * i + j : 3 * i + j + 1, start : start + step] for i in range(3)]
            sums.append(
                body[0:rows] * k[0] + body[1 : rows + 1] * k[1] + body[2 : rows + 2] * k[2]
            )
            if j != 1:
                part = side[:16] if j == 0 else side[16:]
                edge = part[0:rows] * k[0] + part[1 : rows + 1] * k[1] + part[2 : rows + 2] * k[2]
                edges.append(edge.reshape(rows, 1, step))
        left = jnp.where(first_col, edges[0], pltpu.roll(sums[0], 1, 1))
        right = jnp.where(last_col, edges[1], pltpu.roll(sums[2], breadth - 1, 1))
        spatial = gelu(sums[1] + left + right).reshape(rows * breadth, step).astype(BF16)
        part = dot(spatial, conv_reduce[start : start + step, :])
        projected = part if projected is None else projected + part
    after = main + projected.reshape(rows, breadth, channels)
    per_row = breadth // WIN
    x = jnp.concatenate(
        [
            after[:, v * WIN : (v + 1) * WIN].reshape(rows * WIN, channels)
            for v in range(per_row)
        ],
        axis=0,
    )

    out = section(
        x, lambda w: flags_ref[u, w].astype(F32), attend, merge, expand, reduce_weight
    )
    owners, _, owned, span, _ = out_ref.shape
    repeat = span // WIN
    for r in range(owners):
        for c in range(col_count):
            pieces = [
                out[(h * col_count + c) * WIN * WIN :][: WIN * WIN]
                .reshape(WIN, WIN, channels)[r * owned : (r + 1) * owned]
                for h in range(repeat)
            ]
            out_ref[r, c] = jnp.concatenate(pieces, axis=1).astype(BF16)


def grid_kernel(flags_ref, x_ref, attend, merge, expand, reduce_weight, out_ref):
    p, i = pl.program_id(0), pl.program_id(1)
    shape = x_ref.shape
    channels = shape[-1]
    tokens = WIN * GRID * GRID
    x = x_ref[...].reshape(tokens, channels)
    row = lax.broadcasted_iota(jnp.int32, (tokens, tokens), 0)
    col = lax.broadcasted_iota(jnp.int32, (tokens, tokens), 1)
    per = GRID * GRID
    order = jnp.where(col == (row % per) * WIN + row // per, 1.0, 0.0).astype(BF16)
    back = jnp.where(row == (col % per) * WIN + col // per, 1.0, 0.0).astype(BF16)
    out = section(
        dot(order, x),
        lambda w: flags_ref[p, i, w].astype(F32),
        attend,
        merge,
        expand,
        reduce_weight,
    )
    out_ref[...] = dot(back, out.astype(BF16)).astype(BF16).reshape(shape)


def whole(array):
    return pl.BlockSpec(array.shape, lambda *_: (0,) * array.ndim)


def shift(array, axis, up):
    size = lax.axis_size(axis)
    pairs = [(i, i + 1) for i in range(size - 1)]
    return lax.ppermute(array, axis, pairs if up else [(j, i) for i, j in pairs])


PARAMS = pltpu.CompilerParams(vmem_limit_bytes=56 << 20)


def conv_and_blocks(features, weights, flags, row_count, col_count):
    height, breadth, channels = features.shape
    bands = height // WIN
    top = shift(features[height - 1 :], "row", True)
    bottom = shift(features[:1], "row", False)
    edge_columns = [
        jnp.concatenate([top[:, c], features[:, c], bottom[:, c]], axis=0) for c in (0, breadth - 1)
    ]
    left = shift(edge_columns[1], "col", True)
    right = shift(edge_columns[0], "col", False)
    tall = WIN + 2
    gap = jnp.zeros((16 - tall, channels), BF16)
    sides = jnp.stack(
        [
            jnp.concatenate(
                [left[u * WIN : u * WIN + tall], gap, right[u * WIN : u * WIN + tall], gap]
            )
            for u in range(bands)
        ]
    )
    step_rows = height // row_count if height // row_count <= WIN else WIN
    owners = WIN // step_rows
    span = breadth // col_count
    in_specs = [
        pl.BlockSpec((WIN, breadth, channels), lambda u, f: (u, 0, 0)),
        pl.BlockSpec((1, breadth, channels), lambda u, f: (jnp.maximum(u * WIN - 1, 0), 0, 0)),
        pl.BlockSpec(
            (1, breadth, channels), lambda u, f: (jnp.minimum(u * WIN + WIN, height - 1), 0, 0)
        ),
        whole(top),
        whole(bottom),
        pl.BlockSpec((1, 32, channels), lambda u, f: (u, 0, 0)),
    ] + [whole(w) for w in weights]
    return pl.pallas_call(
        functools.partial(band_kernel, col_count),
        out_shape=jax.ShapeDtypeStruct((row_count, col_count, step_rows, span, channels), BF16),
        grid_spec=pltpu.PrefetchScalarGridSpec(
            num_scalar_prefetch=1,
            grid=(bands,),
            in_specs=in_specs,
            out_specs=pl.BlockSpec(
                (owners, col_count, step_rows, span, channels), lambda u, f: (u, 0, 0, 0, 0)
            ),
        ),
        compiler_params=PARAMS,
        name="conv_and_blocks",
    )(flags, features, features, features, top, bottom, sides, *weights)


def grid_section(arrived, weights, flags):
    shape = arrived.shape
    a, p, b, i, span, channels = shape
    spec = pl.BlockSpec((a, 1, b, 1, span, channels), lambda p, i, f: (0, p, 0, i, 0, 0))
    return pl.pallas_call(
        grid_kernel,
        out_shape=jax.ShapeDtypeStruct(shape, BF16),
        grid_spec=pltpu.PrefetchScalarGridSpec(
            num_scalar_prefetch=1,
            grid=(p, i),
            in_specs=[spec] + [whole(w) for w in weights],
            out_specs=spec,
        ),
        compiler_params=PARAMS,
        name="grid_section",
    )(flags, arrived, *weights)


def exchange(array):
    return lax.all_to_all(array, ("row", "col"), split_axis=0, concat_axis=0, tiled=True)


def on_device(
    features,
    conv_expand,
    conv_kernel,
    conv_reduce,
    block_attend,
    block_merge,
    block_expand,
    block_reduce,
    grid_attend,
    grid_merge,
    grid_expand,
    grid_reduce,
    block_valid,
    grid_valid,
):
    height, breadth, channels = features.shape
    rows, cols = lax.axis_size("row"), lax.axis_size("col")
    sending = conv_and_blocks(
        features,
        (
            conv_expand,
            conv_kernel,
            conv_reduce,
            block_attend,
            block_merge,
            block_expand,
            block_reduce,
        ),
        block_valid,
        rows,
        cols,
    )
    step_rows, span = sending.shape[2:4]
    parity = max(1, rows // GRID)
    arrived = exchange(sending.reshape(rows * cols, step_rows, span, channels))
    finished = grid_section(
        arrived.reshape(rows // parity, parity, cols, step_rows, span, channels),
        (grid_attend, grid_merge, grid_expand, grid_reduce),
        grid_valid.reshape(parity, step_rows, WIN),
    )
    returned = exchange(finished.reshape(rows * cols, step_rows, span, channels))
    spread = returned.reshape(rows, cols, step_rows, span // WIN, WIN, channels)
    return jnp.transpose(spread, (0, 2, 3, 1, 4, 5)).reshape(height, breadth, channels)


def solution(mesh):
    in_specs = (P("row", "col", None),) + (P(),) * 11 + (P("row", "col"), P(None, "row", None, "col"))
    return jax.shard_map(
        on_device,
        mesh=mesh,
        in_specs=in_specs,
        out_specs=P("row", "col", None),
        check_vma=False,
    )
```

time: 614 us -> 241 us (0.39)
  matrix products: 293 us -> 0 us
  Pallas kernels: 0 us -> 113 us
  local copies, waits for them, and re-layouts: 102 us -> 4.23 us
  other arithmetic: 88.9 us -> 0.14 us
  blocking collectives: 52.1 us -> 110 us
  waiting for transfers between devices: 58.3 us -> 1.02 us
    dot_general x12 -> x0, matrix products: 293 us -> none  [the longest x2 82 us: window_section(): jnp.dot(hidden, reduce_weight, preferred_element_type=jnp.float32)]
    pallas_call x0 -> x2, Pallas kernels: none -> 113 us  [the longest x1 67.1 us: conv_and_blocks(): pl.pallas_call(functools.partial(band_kernel, col_count), out_shape=jax.S...]
    all_to_all x1 -> x2, blocking collectives: 52.1 us -> 110 us  [exchange(): lax.all_to_all(array, ('row', 'col'), split_axis=0, concat_axis=0, tiled=...]
    all_to_all x1 -> x0, waiting for transfers between devices: 48.1 us -> none  [to_grid(): lax.all_to_all(flattened, ('row', 'col'), split_axis=0, concat_axis=0, ti...]
    sub x2 -> x0, other arithmetic: 37.6 us -> none  [attend_windows(): probs = jax.nn.softmax(scores, axis=-1).astype(jnp.bfloat16)]
    reshape x4 -> x1, local copies, waits for them, and re-layouts: 39 us -> 1.61 us  [on_device(): spread = returned.reshape(rows, cols, step_rows, span // WIN, WIN, channels)]
    convert_element_type x8 -> x0, local copies, waits for them, and re-layouts: 37 us -> none  [the longest x4 19.1 us: window_section(): windows.astype(jnp.float32)]
    reduce_sum x8 -> x0, other arithmetic: 17.7 us -> none  [the longest x5 11.5 us: layer_norm(): variance = jnp.mean(centred * centred, axis=-1, keepdims=True)]
  transfers between devices with their start and end apart: 5 -> 4, of which waited for: 4 -> 1; matrix products, arithmetic and copies ran while one was open for 0% -> 0% of each run, Pallas kernels for 0% -> 0%
where the time goes in v1:
time: 241 us; the launch traced here: 240 us
  Pallas kernels  113 us (47%)
  blocking collectives  110 us (46%)
  starting transfers between devices  11.7 us (5%)
  local copies, waits for them, and re-layouts  4.23 us (2%)
    all_to_all x2, blocking collectives, exchange(): lax.all_to_all(array, ('row', 'col'), split_axis=0, concat_axis=0, tiled=...  110 us
    pallas_call x1, Pallas kernels, conv_and_blocks(): pl.pallas_call(functools.partial(band_kernel, col_count), out_shape=jax.S...  67.1 us
    pallas_call x1, Pallas kernels, grid_section(): pl.pallas_call(grid_kernel, out_shape=jax.ShapeDtypeStruct(shape, BF16),...  45.5 us
    ppermute x4, starting transfers between devices, shift(): lax.ppermute(array, axis, pairs if up else [(j, i) for i, j in pairs])  11.7 us
  transfers between devices with their start and end apart: 4, of which 1 were waited for; matrix products, arithmetic and copies ran while one was open for 0% of the time, Pallas kernels for 0%

profile of v1, /device:TPU:1, one launch (start us, length us, event | category | flops | bytes accessed | tf_op | source)
XLA Modules:
  0.0 240.1 jit_solution(13630853564159056166)
XLA Ops:
  0.0 0.8 fusion.17
  0.8 2.0 collective-permute-start.1
  2.7 4.5 %collective-permute-start = (bf16[1,64,256]{2,1,0:T(8,128)(2,1)S(1)}, bf16[1,64,256]{2,1,0:T(8,128)(2,1)S(1)}, u32[]{:S(2)}, u32[]{:S(2)}) collective-permute-start(bf16[1,64,256]{2,1,0:T(8,128)(2,1)S(1)} %get-tuple-element.8), channel_id=1, source_target_pairs={{0,4},{4,8},{8,12},{12,16},{16,20},{20,24},{24,28},{1,5},{5,9},{9,... | collective-permute-start | bytes 98312 | tf_op jit(solution)/shard_map/ppermute | solution.py:206
  7.2 1.1 fusion.16
  8.4 0.0 collective-permute-done.1.bottom_ref
  8.4 0.0 copy-start.1
  8.4 0.0 collective-permute-done.top_ref
  8.4 0.0 copy-start.2
  8.5 1.3 collective-permute-start.3
  9.8 4.0 %collective-permute-start.2 = (bf16[66,256]{1,0:T(8,128)(2,1)S(1)}, bf16[66,256]{1,0:T(8,128)(2,1)S(1)}, u32[]{:S(2)}, u32[]{:S(2)}) collective-permute-start(bf16[66,256]{1,0:T(8,128)(2,1)S(1)} %pad_maximum_fusion.16), channel_id=1, source_target_pairs={{0,1},{1,2},{2,3},{4,5},{5,6},{6,7},{8,9},{9,10},{10,11},{12,13},{... | collective-permute-start | bytes 101384 | tf_op jit(solution)/shard_map/ppermute | solution.py:206
  13.8 0.0 collective-permute-done.3
  13.8 1.0 collective-permute-done.2
  15.0 0.0 copy-done.1
  15.0 0.0 copy-done.2
  15.0 0.0 copy-start
  15.0 0.6 copy-done
  15.7 67.1 %conv_and_blocks.1 = bf16[8,4,8,16,256]{4,3,2,1,0:T(8,128)(2,1)} custom-call(s32[8,8]{1,0:T(8,128)} %flags_ref.1, bf16[64,64,256]{2,1,0:T(8,128)(2,1)} %below_ref.1, bf16[64,64,256]{2,1,0:T(8,128)(2,1)} %below_ref.1, bf16[64,64,256]{2,1,0:T(8,128)(2,1)} %below_ref.1, bf16[1,64,256]{2,1,0:T(8,128)(2,1)} %copy-done.2, bf16[1,64,256]{2,1,0:T(8,128)(2,1)} %copy-done.1, ...), custom_call_target="tpu_custom_call" | custom-call | tf_op jit(solution)/shard_map/conv_and_blocks/pallas_call | solution.py:245
  82.8 58.2 %all_to_all.10 = bf16[32,8,16,256]{3,2,1,0:T(8,128)(2,1)} all-to-all(bf16[32,8,16,256]{3,2,1,0:T(8,128)(2,1)} %bitcast.54), channel_id=1, replica_groups=mesh['row'=8,'col'=4] {'row','col'}, dimensions={0} | all-to-all | bytes 4194304 | tf_op jit(solution)/shard_map/all_to_all | solution.py:280
  141.0 45.5 %grid_section.1 = bf16[8,1,4,8,16,256]{5,4,3,2,1,0:T(8,128)(2,1)} custom-call(s32[1,8,8]{2,1,0:T(8,128)} %bitcast.60, bf16[8,1,4,8,16,256]{5,4,3,2,1,0:T(8,128)(2,1)} %bitcast.55, bf16[256,768]{1,0:T(8,128)(2,1)} %attend.3, bf16[256,256]{1,0:T(8,128)(2,1)} %merge.3, bf16[256,1024]{1,0:T(8,128)(2,1)} %expand.3, bf16[1024,256]{1,0:T(8,128)(2,1)} %reduce_weight.3), custom_call_target="tpu_custom_call" | custom-call | tf_op jit(solution)/shard_map/grid_section/pallas_call | solution.py:265
  186.5 52.0 %all_to_all.11 = bf16[32,8,16,256]{3,2,1,0:T(8,128)(2,1)S(1)} all-to-all(bf16[32,8,16,256]{3,2,1,0:T(8,128)(2,1)} %bitcast.56), channel_id=1, replica_groups=mesh['row'=8,'col'=4] {'row','col'}, dimensions={0} | all-to-all | bytes 4194304 | tf_op jit(solution)/shard_map/all_to_all | solution.py:280
  238.5 1.6 copy.17
  (17 shorter events, 0.2 us)
Async XLA Ops:
  0.8 7.6 %collective-permute-start.1 = (bf16[1,64,256]{2,1,0:T(8,128)(2,1)S(1)}, bf16[1,64,256]{2,1,0:T(8,128)(2,1)S(1)}, u32[]{:S(2)}, u32[]{:S(2)}) collective-permute-start(bf16[1,64,256]{2,1,0:T(8,128)(2,1)S(1)} %get-tuple-element.7), channel_id=1, source_target_pairs={{4,0},{8,4},{12,8},{16,12},{20,16},{24,20},{28,24},{5,1},{9,5},{13... | collective-permute-start | bytes 98312 | tf_op jit(solution)/shard_map/ppermute | solution.py:206
  2.7 5.7 %collective-permute-start = (bf16[1,64,256]{2,1,0:T(8,128)(2,1)S(1)}, bf16[1,64,256]{2,1,0:T(8,128)(2,1)S(1)}, u32[]{:S(2)}, u32[]{:S(2)}) collective-permute-start(bf16[1,64,256]{2,1,0:T(8,128)(2,1)S(1)} %get-tuple-element.8), channel_id=1, source_target_pairs={{0,4},{4,8},{8,12},{12,16},{16,20},{20,24},{24,28},{1,5},{5,9},{9,... | collective-permute-start | bytes 98312 | tf_op jit(solution)/shard_map/ppermute | solution.py:206
  8.4 6.6 %copy-start.1 = (bf16[1,64,256]{2,1,0:T(8,128)(2,1)}, bf16[1,64,256]{2,1,0:T(8,128)(2,1)S(1)}, u32[]{:S(2)}) copy-start(bf16[1,64,256]{2,1,0:T(8,128)(2,1)S(1)} %collective-permute-done.1.bottom_ref) | copy-start | bytes 98308
  8.4 6.6 %copy-start.2 = (bf16[1,64,256]{2,1,0:T(8,128)(2,1)}, bf16[1,64,256]{2,1,0:T(8,128)(2,1)S(1)}, u32[]{:S(2)}) copy-start(bf16[1,64,256]{2,1,0:T(8,128)(2,1)S(1)} %collective-permute-done.top_ref) | copy-start | bytes 98308
  8.5 5.3 %collective-permute-start.3 = (bf16[66,256]{1,0:T(8,128)(2,1)S(1)}, bf16[66,256]{1,0:T(8,128)(2,1)S(1)}, u32[]{:S(2)}, u32[]{:S(2)}) collective-permute-start(bf16[66,256]{1,0:T(8,128)(2,1)S(1)} %pad_maximum_fusion.17), channel_id=1, source_target_pairs={{1,0},{2,1},{3,2},{5,4},{6,5},{7,6},{9,8},{10,9},{11,10},{13,12},{... | collective-permute-start | bytes 101384 | tf_op jit(solution)/shard_map/ppermute | solution.py:206
  9.8 5.0 %collective-permute-start.2 = (bf16[66,256]{1,0:T(8,128)(2,1)S(1)}, bf16[66,256]{1,0:T(8,128)(2,1)S(1)}, u32[]{:S(2)}, u32[]{:S(2)}) collective-permute-start(bf16[66,256]{1,0:T(8,128)(2,1)S(1)} %pad_maximum_fusion.16), channel_id=1, source_target_pairs={{0,1},{1,2},{2,3},{4,5},{5,6},{6,7},{8,9},{9,10},{10,11},{12,13},{... | collective-permute-start | bytes 101384 | tf_op jit(solution)/shard_map/ppermute | solution.py:206
  15.0 0.7 copy-start

commit v2 on v1

v2 whole, which is shorter than its diff:
```python
import functools

import jax
import jax.numpy as jnp
from jax import lax
from jax.experimental import pallas as pl
from jax.experimental.pallas import tpu as pltpu
from jax.sharding import PartitionSpec as P

HEADS = 8
WIN = 8
GRID = 8
PER = 64
EPSILON = 1e-05
LANES = 128
F32 = jnp.float32
BF16 = jnp.bfloat16
CHUNKS = 2
STEP_BANDS = 2


def dot(a, b):
    return jnp.dot(a, b, preferred_element_type=F32)


def dot_nt(a, b):
    return lax.dot_general(a, b, (((1,), (1,)), ((), ())), preferred_element_type=F32)


def gelu(x):
    return 0.5 * x * (1.0 + lax.erf(x * 0.7071067811865476))


def layer_norm(x):
    channels = x.shape[1]
    average = jnp.full((channels, LANES), 1.0 / channels, BF16)
    rounded = x.astype(BF16)
    mean = dot(rounded, average)
    wide = rounded.astype(F32)
    parts = [wide[:, s : s + LANES] - mean for s in range(0, channels, LANES)]
    squares = jnp.concatenate([(part * part).astype(BF16) for part in parts], axis=1)
    factor = lax.rsqrt(dot(squares, average) + EPSILON)
    return jnp.concatenate([(part * factor).astype(BF16) for part in parts], axis=1)


def attention(packed, count):
    channels = packed.shape[1] // 3
    head_width = channels // HEADS
    per_group = LANES // head_width
    groups = channels // LANES
    scale = head_width ** (-0.5) * 1.4426950408889634
    lane = lax.broadcasted_iota(jnp.int32, (1, LANES), 1)
    masks = [jnp.where(lane // head_width == h, 1.0, 0.0).astype(BF16) for h in range(per_group)]
    low = lane < PER
    row = lax.broadcasted_iota(jnp.int32, (per_group * PER, LANES), 0)
    col = lax.broadcasted_iota(jnp.int32, (per_group * PER, LANES), 1)
    ones = jnp.where(row // PER == col // head_width, 1.0, 0.0).astype(BF16)

    def piece(kind, w, g):
        start = kind * channels + g * LANES
        return packed[w * PER : (w + 1) * PER, start : start + LANES]

    def by_head(x):
        return jnp.concatenate([x * m for m in masks], axis=0)

    items = [(w, g) for g in range(groups) for w in range(count)]
    scores = [dot_nt(piece(0, w, g), by_head(piece(1, w, g))) for w, g in items]
    weights = []
    for s in scores:
        parts = []
        for p in range(per_group * PER // LANES):
            sp = s[:, p * LANES : (p + 1) * LANES]
            m0 = jnp.max(jnp.where(low, sp, -jnp.inf), axis=-1, keepdims=True)
            m1 = jnp.max(jnp.where(low, -jnp.inf, sp), axis=-1, keepdims=True)
            parts.append(jnp.exp2((sp - jnp.where(low, m0, m1)) * scale).astype(BF16))
        weights.append(jnp.concatenate(parts, axis=1))
    total = dot(jnp.concatenate(weights, axis=0), ones)
    tops = [dot(e, by_head(piece(2, w, g))) for (w, g), e in zip(items, weights)]
    mixed = (jnp.concatenate(tops, axis=0) / total).astype(BF16)
    size = count * PER
    return jnp.concatenate([mixed[g * size : (g + 1) * size] for g in range(groups)], axis=1)


def section(x, flags, attend, merge, expand, reduce_weight):
    count = x.shape[0] // PER

    def gated(base, update):
        return jnp.concatenate(
            [
                base[w * PER : (w + 1) * PER] + flags[w] * update[w * PER : (w + 1) * PER]
                for w in range(count)
            ],
            axis=0,
        )

    packed = dot(layer_norm(x), attend[...]).astype(BF16)
    attended = gated(x, dot(attention(packed, count), merge[...]))
    normed = layer_norm(attended)
    hidden_width = expand.shape[1]
    step = min(256, hidden_width)
    reduced = None
    for start in range(0, hidden_width, step):
        hidden = gelu(dot(normed, expand[:, start : start + step])).astype(BF16)
        part = dot(hidden, reduce_weight[start : start + step, :])
        reduced = part if reduced is None else reduced + part
    return gated(attended, reduced)


def mbconv(main, above, below, sides, conv_expand, conv_kernel, conv_reduce):
    rows, breadth, channels = main.shape
    inner = (rows + 2) * breadth
    side_rows = sides.shape[0] // 2
    x = jnp.concatenate([above, main, below], axis=0).reshape(inner, channels)
    normed = layer_norm(jnp.concatenate([x, sides], axis=0))
    width = conv_expand.shape[1]
    step = min(256, width)
    column = lax.broadcasted_iota(jnp.int32, (1, breadth, 1), 1)
    first_col = column == 0
    last_col = column == breadth - 1
    taps = conv_kernel[...].astype(F32)
    projected = None
    for start in range(0, width, step):
        e = gelu(dot(normed, conv_expand[:, start : start + step]))
        body = e[:inner].reshape(rows + 2, breadth, step)
        side = e[inner:]
        sums, edges = [], []
        for j in range(3):
            k = [taps[3 * i + j : 3 * i + j + 1, start : start + step] for i in range(3)]
            sums.append(
                body[0:rows] * k[0] + body[1 : rows + 1] * k[1] + body[2 : rows + 2] * k[2]
            )
            if j != 1:
                part = side[:side_rows] if j == 0 else side[side_rows:]
                edge = part[0:rows] * k[0] + part[1 : rows + 1] * k[1] + part[2 : rows + 2] * k[2]
                edges.append(edge.reshape(rows, 1, step))
        left = jnp.where(first_col, edges[0], pltpu.roll(sums[0], 1, 1))
        right = jnp.where(last_col, edges[1], pltpu.roll(sums[2], breadth - 1, 1))
        spatial = gelu(sums[1] + left + right).reshape(rows * breadth, step).astype(BF16)
        part = dot(spatial, conv_reduce[start : start + step, :])
        projected = part if projected is None else projected + part
    return main + projected.reshape(rows, breadth, channels)


def band_kernel(
    first_band,
    direct,
    flags_ref,
    main_ref,
    above_ref,
    below_ref,
    top_ref,
    bottom_ref,
    sides_ref,
    conv_expand,
    conv_kernel,
    conv_reduce,
    attend,
    merge,
    expand,
    reduce_weight,
    out_ref,
):
    rows, breadth, channels = main_ref.shape
    bands, per_row = rows // WIN, breadth // WIN
    step = pl.program_id(0)
    first_band = first_band + step * bands
    last_band = flags_ref.shape[0] - bands
    above = jnp.where(first_band == 0, top_ref[...].astype(F32), above_ref[...].astype(F32))
    below = jnp.where(
        first_band == last_band, bottom_ref[...].astype(F32), below_ref[...].astype(F32)
    )
    after = mbconv(
        main_ref[...].astype(F32),
        above,
        below,
        sides_ref[0].astype(F32),
        conv_expand,
        conv_kernel,
        conv_reduce,
    )
    windows = [(t, v) for t in range(bands) for v in range(per_row)]
    x = jnp.concatenate(
        [
            after[t * WIN : (t + 1) * WIN, v * WIN : (v + 1) * WIN].reshape(PER, channels)
            for t, v in windows
        ],
        axis=0,
    )
    flags = [flags_ref[first_band + t, v].astype(F32) for t, v in windows]
    out = section(x, flags, attend, merge, expand, reduce_weight)
    square = {
        tv: out[n * PER : (n + 1) * PER].reshape(WIN, WIN, channels)
        for n, tv in enumerate(windows)
    }
    if direct:
        cols = out_ref.shape[1]
        for t in range(bands):
            for c in range(cols):
                pieces = [square[t, v] for v in range(c, per_row, cols)]
                out_ref[:, c, t] = jnp.concatenate(pieces, axis=1).astype(BF16)
    else:
        for t in range(bands):
            pieces = [square[t, v] for v in range(per_row)]
            out_ref[t * WIN : (t + 1) * WIN] = jnp.concatenate(pieces, axis=1).astype(BF16)


def grid_kernel(first_band, direct, flags_ref, x_ref, attend, merge, expand, reduce_weight, out_ref):
    channels = x_ref.shape[-1]
    tokens = WIN * PER
    first_band = first_band + pl.program_id(0) * STEP_BANDS
    if direct:
        bands = x_ref.shape[1]
        row = lax.broadcasted_iota(jnp.int32, (tokens, tokens), 0)
        col = lax.broadcasted_iota(jnp.int32, (tokens, tokens), 1)
        order = jnp.where(col == (row % PER) * WIN + row // PER, 1.0, 0.0).astype(BF16)
        back = jnp.where(row == (col % PER) * WIN + col // PER, 1.0, 0.0).astype(BF16)
        x = [dot(order, x_ref[:, t].reshape(tokens, channels)) for t in range(bands)]
    else:
        bands = x_ref.shape[0]
        x = [x_ref[t].astype(F32) for t in range(bands)]
    flags = [flags_ref[first_band + t, w].astype(F32) for t in range(bands) for w in range(WIN)]
    out = section(jnp.concatenate(x, axis=0), flags, attend, merge, expand, reduce_weight)
    for t in range(bands):
        part = out[t * tokens : (t + 1) * tokens].astype(BF16)
        if direct:
            out_ref[:, t] = dot(back, part).astype(BF16).reshape(out_ref[:, t].shape)
        else:
            out_ref[t] = part


def whole(array):
    return pl.BlockSpec(array.shape, lambda *_: (0,) * array.ndim)


def shift(array, axis, up):
    size = lax.axis_size(axis)
    pairs = [(i, i + 1) for i in range(size - 1)]
    return lax.ppermute(array, axis, pairs if up else [(j, i) for i, j in pairs])


PARAMS = pltpu.CompilerParams(vmem_limit_bytes=60 << 20)


def along(shape, axis, size):
    block = shape[:axis] + (size,) + shape[axis + 1 :]
    return pl.BlockSpec(
        block, lambda i, f: (0,) * axis + (i,) + (0,) * (len(shape) - axis - 1)
    )


def call(kernel, steps, flags, specs, arrays, shape, out_spec, name):
    return pl.pallas_call(
        kernel,
        out_shape=jax.ShapeDtypeStruct(shape, BF16),
        grid_spec=pltpu.PrefetchScalarGridSpec(
            num_scalar_prefetch=1, grid=(steps,), in_specs=specs, out_specs=out_spec
        ),
        compiler_params=PARAMS,
        name=name,
    )(flags, *arrays)


def feature_halo(features, beside):
    height, breadth, _ = features.shape
    top = shift(features[height - 1 :], "row", True)
    bottom = shift(features[:1], "row", False)
    edge_columns = [
        jnp.concatenate([top[:, c], features[:, c], bottom[:, c]], axis=0) for c in (0, breadth - 1)
    ]
    edge_columns, beside = lax.optimization_barrier((edge_columns, beside))
    left = shift(edge_columns[1], "col", True)
    right = shift(edge_columns[0], "col", False)
    return top, bottom, left, right, beside


def exchange(array):
    return lax.all_to_all(array, ("row", "col"), split_axis=0, concat_axis=0, tiled=True)


def on_device(
    features,
    conv_expand,
    conv_kernel,
    conv_reduce,
    block_attend,
    block_merge,
    block_expand,
    block_reduce,
    grid_attend,
    grid_merge,
    grid_expand,
    grid_reduce,
    block_valid,
    grid_valid,
):
    height, breadth, channels = features.shape
    rows, cols = lax.axis_size("row"), lax.axis_size("col")
    devices = rows * cols
    parity = rows // GRID
    repeat = breadth // (WIN * cols)
    part = WIN // parity
    direct = parity == 1
    per_chunk = height // WIN // CHUNKS
    tall = per_chunk * WIN

    me = lax.axis_index("row")
    gathered = lax.all_gather(grid_valid[:, :, 0, :], "row", axis=1, tiled=True)
    by_band = gathered.reshape(parity, height // WIN, WIN, WIN)
    mine = lax.dynamic_index_in_dim(by_band, me // parity, 2, keepdims=False)
    mine = lax.dynamic_slice_in_dim(mine, (me % parity) * part, part, 2)
    grid_flags = jnp.transpose(mine, (1, 0, 2)).reshape(height // WIN, WIN)

    top, bottom, left, right, grid_flags = feature_halo(features, grid_flags)
    conv_weights = (conv_expand, conv_kernel, conv_reduce)
    block_weights = (block_attend, block_merge, block_expand, block_reduce)
    grid_weights = (grid_attend, grid_merge, grid_expand, grid_reduce)
    steps = per_chunk // STEP_BANDS
    step_rows = STEP_BANDS * WIN
    padded = -(-(step_rows + 2) // 8) * 8
    gap = jnp.zeros((padded - step_rows - 2, channels), BF16)
    row_block = (1, breadth, channels)

    outputs = []
    for k in range(CHUNKS):
        low = k * tall
        sides = jnp.stack(
            [
                jnp.concatenate([left[r : r + step_rows + 2], gap, right[r : r + step_rows + 2], gap])
                for r in range(low, low + tall, step_rows)
            ]
        )
        arrays = [features, features, features, top, bottom, sides, *conv_weights, *block_weights]

        def row_at(offset, k=k):
            def index(i, f):
                row = (k * steps + i) * step_rows + offset
                return jnp.clip(row, 0, height - 1), 0, 0

            return pl.BlockSpec(row_block, index)

        specs = [
            pl.BlockSpec((step_rows, breadth, channels), lambda i, f, k=k: (k * steps + i, 0, 0)),
            row_at(-1),
            row_at(step_rows),
            whole(top),
            whole(bottom),
            along(sides.shape, 0, 1),
        ] + [whole(a) for a in arrays[6:]]
        if direct:
            shape = (rows, cols, per_chunk, repeat * WIN, channels)
            out_spec = along(shape, 2, STEP_BANDS)
        else:
            shape = (tall, breadth, channels)
            out_spec = along(shape, 0, step_rows)
        sending = call(
            functools.partial(band_kernel, k * per_chunk, direct),
            steps,
            block_valid,
            specs,
            arrays,
            shape,
            out_spec,
            "conv_and_blocks",
        )
        if not direct:
            split = sending.reshape(per_chunk, WIN, repeat, cols, parity, part, channels)
            sending = jnp.transpose(split, (1, 4, 3, 0, 2, 5, 6))
        arrived = exchange(sending.reshape(devices, per_chunk, repeat * part, channels))
        if not direct:
            split = arrived.reshape(GRID, parity, cols, per_chunk, repeat, part, channels)
            arrived = jnp.transpose(split, (3, 1, 5, 0, 2, 4, 6))
            arrived = arrived.reshape(per_chunk, WIN * PER, channels)
        arrays = [arrived, *grid_weights]
        spec = along(arrived.shape, 1 if direct else 0, STEP_BANDS)
        finished = call(
            functools.partial(grid_kernel, k * per_chunk, direct),
            steps,
            grid_flags,
            [spec] + [whole(a) for a in grid_weights],
            arrays,
            arrived.shape,
            spec,
            "grid_section",
        )
        if not direct:
            split = finished.reshape(per_chunk, parity, part, GRID, cols, repeat, channels)
            finished = jnp.transpose(split, (3, 1, 4, 0, 5, 2, 6))
        returned = exchange(finished.reshape(devices, per_chunk, repeat * part, channels))
        split = returned.reshape(WIN, parity, cols, per_chunk, repeat, part, channels)
        spread = jnp.transpose(split, (3, 0, 4, 2, 1, 5, 6))
        outputs.append(spread.reshape(tall, breadth, channels))
    return jnp.concatenate(outputs, axis=0)


def solution(mesh):
    in_specs = (P("row", "col", None),) + (P(),) * 11
    in_specs += (P("row", "col"), P(None, "row", None, "col"))
    return jax.shard_map(
        on_device,
        mesh=mesh,
        in_specs=in_specs,
        out_specs=P("row", "col", None),
        check_vma=False,
    )
```

time: 241 us -> 173 us (0.72)
  blocking collectives: 110 us -> 10.4 us
  waiting for transfers between devices: 1.02 us -> 60.3 us
  Pallas kernels: 113 us -> 70.2 us
  starting transfers between devices: 11.7 us -> 25.6 us
  other arithmetic: 0.14 us -> 2.81 us
    all_to_all x2 -> x0, blocking collectives: 110 us -> none  [exchange(): lax.all_to_all(array, ('row', 'col'), split_axis=0, concat_axis=0, tiled=...]
    all_to_all x0 -> x4, waiting for transfers between devices: none -> 56.9 us  [exchange(): lax.all_to_all(array, ('row', 'col'), split_axis=0, concat_axis=0, tiled=...]
    pallas_call x2 -> x4, Pallas kernels: 113 us -> 70.2 us  [call(): pl.pallas_call(kernel, out_shape=jax.ShapeDtypeStruct(shape, BF16), grid_...]
    all_to_all x0 -> x4, starting transfers between devices: none -> 14.7 us  [exchange(): lax.all_to_all(array, ('row', 'col'), split_axis=0, concat_axis=0, tiled=...]
    all_gather x0 -> x1, blocking collectives: none -> 10.4 us  [on_device(): gathered = lax.all_gather(grid_valid[:, :, 0, :], 'row', axis=1, tiled=True)]
  transfers between devices with their start and end apart: 4 -> 8, of which waited for: 1 -> 5; matrix products, arithmetic and copies ran while one was open for 0% -> 1% of each run, Pallas kernels for 0% -> 28%
where the time goes in v2:
time: 173 us; the launch traced here: 172 us
  Pallas kernels  70.2 us (41%)
  waiting for transfers between devices  60.3 us (35%)
  starting transfers between devices  25.6 us (15%)
  blocking collectives  10.4 us (6%)
  local copies, waits for them, and re-layouts  2.83 us (2%)
  other arithmetic  2.81 us (2%)
    pallas_call x4, Pallas kernels, call(): pl.pallas_call(kernel, out_shape=jax.ShapeDtypeStruct(shape, BF16), grid_...  70.2 us
    all_to_all x4, waiting for transfers between devices, exchange(): lax.all_to_all(array, ('row', 'col'), split_axis=0, concat_axis=0, tiled=...  56.9 us
    all_to_all x4, starting transfers between devices, exchange(): lax.all_to_all(array, ('row', 'col'), split_axis=0, concat_axis=0, tiled=...  14.7 us
    ppermute x4, starting transfers between devices, shift(): lax.ppermute(array, axis, pairs if up else [(j, i) for i, j in pairs])  10.9 us
    all_gather x1, blocking collectives, on_device(): gathered = lax.all_gather(grid_valid[:, :, 0, :], 'row', axis=1, tiled=True)  10.4 us
  transfers between devices with their start and end apart: 8, of which 5 were waited for; matrix products, arithmetic and copies ran while one was open for 1% of the time, Pallas kernels for 28%

profile of v2, /device:TPU:1, one launch (start us, length us, event | category | flops | bytes accessed | tf_op | source)
XLA Modules:
  0.0 172.3 jit_solution(8787619989451656139)
XLA Ops:
  0.0 0.8 fusion.9
  0.8 4.5 %collective-permute-start = (bf16[1,64,256]{2,1,0:T(8,128)(2,1)S(1)}, bf16[1,64,256]{2,1,0:T(8,128)(2,1)S(1)}, u32[]{:S(2)}, u32[]{:S(2)}) collective-permute-start(bf16[1,64,256]{2,1,0:T(8,128)(2,1)S(1)} %get-tuple-element.13), channel_id=1, source_target_pairs={{0,4},{4,8},{8,12},{12,16},{16,20},{20,24},{24,28},{1,5},{5,9},{9,... | collective-permute-start | bytes 98312 | tf_op jit(solution)/shard_map/ppermute | solution.py:238
  5.3 1.9 %collective-permute-start.1 = (bf16[1,64,256]{2,1,0:T(8,128)(2,1)S(1)}, bf16[1,64,256]{2,1,0:T(8,128)(2,1)S(1)}, u32[]{:S(2)}, u32[]{:S(2)}) collective-permute-start(bf16[1,64,256]{2,1,0:T(8,128)(2,1)S(1)} %get-tuple-element.14), channel_id=1, source_target_pairs={{4,0},{8,4},{12,8},{16,12},{20,16},{24,20},{28,24},{5,1},{9,5},{13... | collective-permute-start | bytes 98312 | tf_op jit(solution)/shard_map/ppermute | solution.py:238
  7.2 1.1 fusion.8
  8.4 10.4 %all-gather = s32[1,64,1,8]{3,2,0,1:T(1,128)S(1)} all-gather(s32[1,8,1,8]{3,2,0,1:T(1,128)} %bitcast.48), channel_id=2, replica_groups=mesh['row'=8,'col'=4] {'row'}, dimensions={1}, use_global_device_ids=true | all-gather | bytes 2304 | tf_op jit(solution)/shard_map/all_gather | solution.py:307
  18.8 0.6 constant_dynamic-slice_fusion
  19.4 0.0 collective-permute-done.top_ref
  19.4 0.0 copy-start.2
  19.4 0.0 collective-permute-done.1.bottom_ref
  19.5 0.0 copy-start.3
  19.5 3.2 %collective-permute-start.2 = (bf16[66,256]{1,0:T(8,128)(2,1)S(1)}, bf16[66,256]{1,0:T(8,128)(2,1)S(1)}, u32[]{:S(2)}, u32[]{:S(2)}) collective-permute-start(bf16[66,256]{1,0:T(8,128)(2,1)S(1)} %get-tuple-element.9), channel_id=1, source_target_pairs={{0,1},{1,2},{2,3},{4,5},{5,6},{6,7},{8,9},{9,10},{10,11},{12,13},{... | collective-permute-start | bytes 101384 | tf_op jit(solution)/shard_map/ppermute | solution.py:238
  22.7 1.3 collective-permute-start.3
  24.0 0.0 collective-permute-done.2
  24.1 3.4 %collective-permute-done.3 = bf16[66,256]{1,0:T(8,128)(2,1)S(1)} collective-permute-done((bf16[66,256]{1,0:T(8,128)(2,1)S(1)}, bf16[66,256]{1,0:T(8,128)(2,1)S(1)}, u32[]{:S(2)}, u32[]{:S(2)}) %collective-permute-start.3) | collective-permute-done | bytes 33824 | tf_op jit(solution)/shard_map/ppermute | solution.py:238
  27.5 0.6 pad_maximum_fusion.10.sides_ref
  28.1 0.0 copy-done.2
  28.1 22.5 %conv_and_blocks.3 = bf16[8,4,4,16,256]{4,3,2,1,0:T(8,128)(2,1)} custom-call(s32[8,8]{1,0:T(8,128)} %flags_ref.3, bf16[64,64,256]{2,1,0:T(8,128)(2,1)} %below_ref.3, bf16[64,64,256]{2,1,0:T(8,128)(2,1)} %below_ref.3, bf16[64,64,256]{2,1,0:T(8,128)(2,1)} %below_ref.3, bf16[1,64,256]{2,1,0:T(8,128)(2,1)} %copy-done.2, bf16[1,64,256]{2,1,0:T(8,128)(2,1)} %copy-done.3, ...), custom_call_target="tpu_custom_call" | custom-call | tf_op jit(solution)/shard_map/conv_and_blocks/pallas_call | solution.py:252
  50.6 5.2 %all-to-all-start.2 = ((bf16[32,4,16,256]{3,2,1,0:T(8,128)(2,1)}), bf16[32,4,16,256]{3,2,1,0:T(8,128)(2,1)S(1)}, u32[]{:S(2)}, u32[]{:S(2)}) async-start(bf16[32,4,16,256]{3,2,1,0:T(8,128)(2,1)} %bitcast.38), calls=%async_computation.2 | async-start | bytes 2097152 | tf_op jit(solution)/shard_map/all_to_all | solution.py:277
  55.8 0.6 pad_maximum_fusion.9.sides_ref
  56.4 22.5 %conv_and_blocks.2 = bf16[8,4,4,16,256]{4,3,2,1,0:T(8,128)(2,1)} custom-call(s32[8,8]{1,0:T(8,128)} %flags_ref.3, bf16[64,64,256]{2,1,0:T(8,128)(2,1)} %below_ref.3, bf16[64,64,256]{2,1,0:T(8,128)(2,1)} %below_ref.3, bf16[64,64,256]{2,1,0:T(8,128)(2,1)} %below_ref.3, bf16[1,64,256]{2,1,0:T(8,128)(2,1)} %copy-done.2, bf16[1,64,256]{2,1,0:T(8,128)(2,1)} %copy-done.3, ...), custom_call_target="tpu_custom_call" | custom-call | tf_op jit(solution)/shard_map/conv_and_blocks/pallas_call | solution.py:252
  78.9 3.3 %all-to-all-done.2.x_ref = bf16[32,4,16,256]{3,2,1,0:T(8,128)(2,1)S(1)} async-done(((bf16[32,4,16,256]{3,2,1,0:T(8,128)(2,1)}), bf16[32,4,16,256]{3,2,1,0:T(8,128)(2,1)S(1)}, u32[]{:S(2)}, u32[]{:S(2)}) %all-to-all-start.2) | async-done | bytes 1048608 | tf_op jit(solution)/shard_map/all_to_all | solution.py:277
  82.2 3.2 %all-to-all-start = ((bf16[32,4,16,256]{3,2,1,0:T(8,128)(2,1)}), bf16[32,4,16,256]{3,2,1,0:T(8,128)(2,1)S(1)}, u32[]{:S(2)}, u32[]{:S(2)}) async-start(bf16[32,4,16,256]{3,2,1,0:T(8,128)(2,1)} %bitcast.37), calls=%async_computation | async-start | bytes 2097152 | tf_op jit(solution)/shard_map/all_to_all | solution.py:277
  85.3 12.6 %grid_section.3 = bf16[32,4,16,256]{3,2,1,0:T(8,128)(2,1)} custom-call(s32[8,8]{1,0:T(8,128)} %bitcast.46, bf16[32,4,16,256]{3,2,1,0:T(8,128)(2,1)} %copy-done, bf16[256,768]{1,0:T(8,128)(2,1)} %attend.7, bf16[256,256]{1,0:T(8,128)(2,1)} %merge.7, bf16[256,1024]{1,0:T(8,128)(2,1)} %expand.7, bf16[1024,256]{1,0:T(8,128)(2,1)} %reduce_weight.7), custom_call_target="tpu_custom_call" | custom-call | tf_op jit(solution)/shard_map/grid_section/pallas_call | solution.py:252
  98.0 13.7 %all-to-all-done.x_ref = bf16[32,4,16,256]{3,2,1,0:T(8,128)(2,1)S(1)} async-done(((bf16[32,4,16,256]{3,2,1,0:T(8,128)(2,1)}), bf16[32,4,16,256]{3,2,1,0:T(8,128)(2,1)S(1)}, u32[]{:S(2)}, u32[]{:S(2)}) %all-to-all-start) | async-done | bytes 1048608 | tf_op jit(solution)/shard_map/all_to_all | solution.py:277
  111.7 3.2 %all-to-all-start.3 = ((bf16[32,4,16,256]{3,2,1,0:T(8,128)(2,1)}), bf16[32,4,16,256]{3,2,1,0:T(8,128)(2,1)S(1)}, u32[]{:S(2)}, u32[]{:S(2)}) async-start(bf16[32,4,16,256]{3,2,1,0:T(8,128)(2,1)} %grid_section.3), calls=%async_computation.3 | async-start | bytes 2097152 | tf_op jit(solution)/shard_map/all_to_all | solution.py:277
  114.8 12.6 %grid_section.2 = bf16[32,4,16,256]{3,2,1,0:T(8,128)(2,1)} custom-call(s32[8,8]{1,0:T(8,128)} %bitcast.47, bf16[32,4,16,256]{3,2,1,0:T(8,128)(2,1)} %copy-done.1, bf16[256,768]{1,0:T(8,128)(2,1)} %attend.7, bf16[256,256]{1,0:T(8,128)(2,1)} %merge.7, bf16[256,1024]{1,0:T(8,128)(2,1)} %expand.7, bf16[1024,256]{1,0:T(8,128)(2,1)} %reduce_weight.7), custom_call_target="tpu_custom_call" | custom-call | tf_op jit(solution)/shard_map/grid_section/pallas_call | solution.py:252
  127.5 13.7 %all-to-all-done.3 = bf16[32,4,16,256]{3,2,1,0:T(8,128)(2,1)S(1)} async-done(((bf16[32,4,16,256]{3,2,1,0:T(8,128)(2,1)}), bf16[32,4,16,256]{3,2,1,0:T(8,128)(2,1)S(1)}, u32[]{:S(2)}, u32[]{:S(2)}) %all-to-all-start.3) | async-done | bytes 1048608 | tf_op jit(solution)/shard_map/all_to_all | solution.py:277
  141.2 3.2 %all-to-all-start.1 = ((bf16[32,4,16,256]{3,2,1,0:T(8,128)(2,1)}), bf16[32,4,16,256]{3,2,1,0:T(8,128)(2,1)S(1)}, u32[]{:S(2)}, u32[]{:S(2)}) async-start(bf16[32,4,16,256]{3,2,1,0:T(8,128)(2,1)} %grid_section.2), calls=%async_computation.1 | async-start | bytes 2097152 | tf_op jit(solution)/shard_map/all_to_all | solution.py:277
  144.4 0.1 copy.31
  144.5 26.2 %all-to-all-done.1 = bf16[32,4,16,256]{3,2,1,0:T(8,128)(2,1)S(1)} async-done(((bf16[32,4,16,256]{3,2,1,0:T(8,128)(2,1)}), bf16[32,4,16,256]{3,2,1,0:T(8,128)(2,1)S(1)}, u32[]{:S(2)}, u32[]{:S(2)}) %all-to-all-start.1) | async-done | bytes 1048608 | tf_op jit(solution)/shard_map/all_to_all | solution.py:277
  170.7 0.1 copy.30
  170.8 1.5 pad_maximum_fusion
  (14 shorter events, 0.1 us)
Async XLA Ops:
  0.8 18.6 %collective-permute-start = (bf16[1,64,256]{2,1,0:T(8,128)(2,1)S(1)}, bf16[1,64,256]{2,1,0:T(8,128)(2,1)S(1)}, u32[]{:S(2)}, u32[]{:S(2)}) collective-permute-start(bf16[1,64,256]{2,1,0:T(8,128)(2,1)S(1)} %get-tuple-element.13), channel_id=1, source_target_pairs={{0,4},{4,8},{8,12},{12,16},{16,20},{20,24},{24,28},{1,5},{5,9},{9,... | collective-permute-start | bytes 98312 | tf_op jit(solution)/shard_map/ppermute | solution.py:238
  5.3 14.2 %collective-permute-start.1 = (bf16[1,64,256]{2,1,0:T(8,128)(2,1)S(1)}, bf16[1,64,256]{2,1,0:T(8,128)(2,1)S(1)}, u32[]{:S(2)}, u32[]{:S(2)}) collective-permute-start(bf16[1,64,256]{2,1,0:T(8,128)(2,1)S(1)} %get-tuple-element.14), channel_id=1, source_target_pairs={{4,0},{8,4},{12,8},{16,12},{20,16},{24,20},{28,24},{5,1},{9,5},{13... | collective-permute-start | bytes 98312 | tf_op jit(solution)/shard_map/ppermute | solution.py:238
  19.4 8.7 %copy-start.2 = (bf16[1,64,256]{2,1,0:T(8,128)(2,1)}, bf16[1,64,256]{2,1,0:T(8,128)(2,1)S(1)}, u32[]{:S(2)}) copy-start(bf16[1,64,256]{2,1,0:T(8,128)(2,1)S(1)} %collective-permute-done.top_ref) | copy-start | bytes 98308
  19.5 8.6 %copy-start.3 = (bf16[1,64,256]{2,1,0:T(8,128)(2,1)}, bf16[1,64,256]{2,1,0:T(8,128)(2,1)S(1)}, u32[]{:S(2)}) copy-start(bf16[1,64,256]{2,1,0:T(8,128)(2,1)S(1)} %collective-permute-done.1.bottom_ref) | copy-start | bytes 98308
  19.5 4.5 %collective-permute-start.2 = (bf16[66,256]{1,0:T(8,128)(2,1)S(1)}, bf16[66,256]{1,0:T(8,128)(2,1)S(1)}, u32[]{:S(2)}, u32[]{:S(2)}) collective-permute-start(bf16[66,256]{1,0:T(8,128)(2,1)S(1)} %get-tuple-element.9), channel_id=1, source_target_pairs={{0,1},{1,2},{2,3},{4,5},{5,6},{6,7},{8,9},{9,10},{10,11},{12,13},{... | collective-permute-start | bytes 101384 | tf_op jit(solution)/shard_map/ppermute | solution.py:238
  22.7 4.7 %collective-permute-start.3 = (bf16[66,256]{1,0:T(8,128)(2,1)S(1)}, bf16[66,256]{1,0:T(8,128)(2,1)S(1)}, u32[]{:S(2)}, u32[]{:S(2)}) collective-permute-start(bf16[66,256]{1,0:T(8,128)(2,1)S(1)} %get-tuple-element.10), channel_id=1, source_target_pairs={{1,0},{2,1},{3,2},{5,4},{6,5},{7,6},{9,8},{10,9},{11,10},{13,12},{... | collective-permute-start | bytes 101384 | tf_op jit(solution)/shard_map/ppermute | solution.py:238
  50.6 31.6 %all-to-all-start.2 = ((bf16[32,4,16,256]{3,2,1,0:T(8,128)(2,1)}), bf16[32,4,16,256]{3,2,1,0:T(8,128)(2,1)S(1)}, u32[]{:S(2)}, u32[]{:S(2)}) async-start(bf16[32,4,16,256]{3,2,1,0:T(8,128)(2,1)} %bitcast.38), calls=%async_computation.2 | async-start | bytes 2097152 | tf_op jit(solution)/shard_map/all_to_all | solution.py:277
  82.1 3.2 %copy-start = (bf16[32,4,16,256]{3,2,1,0:T(8,128)(2,1)}, bf16[32,4,16,256]{3,2,1,0:T(8,128)(2,1)S(1)}, u32[]{:S(2)}) copy-start(bf16[32,4,16,256]{3,2,1,0:T(8,128)(2,1)S(1)} %all-to-all-done.2.x_ref) | copy-start | bytes 3145732
  82.2 29.5 %all-to-all-start = ((bf16[32,4,16,256]{3,2,1,0:T(8,128)(2,1)}), bf16[32,4,16,256]{3,2,1,0:T(8,128)(2,1)S(1)}, u32[]{:S(2)}, u32[]{:S(2)}) async-start(bf16[32,4,16,256]{3,2,1,0:T(8,128)(2,1)} %bitcast.37), calls=%async_computation | async-start | bytes 2097152 | tf_op jit(solution)/shard_map/all_to_all | solution.py:277
  111.7 3.2 %copy-start.1 = (bf16[32,4,16,256]{3,2,1,0:T(8,128)(2,1)}, bf16[32,4,16,256]{3,2,1,0:T(8,128)(2,1)S(1)}, u32[]{:S(2)}) copy-start(bf16[32,4,16,256]{3,2,1,0:T(8,128)(2,1)S(1)} %all-to-all-done.x_ref) | copy-start | bytes 3145732
  111.7 29.5 %all-to-all-start.3 = ((bf16[32,4,16,256]{3,2,1,0:T(8,128)(2,1)}), bf16[32,4,16,256]{3,2,1,0:T(8,128)(2,1)S(1)}, u32[]{:S(2)}, u32[]{:S(2)}) async-start(bf16[32,4,16,256]{3,2,1,0:T(8,128)(2,1)} %grid_section.3), calls=%async_computation.3 | async-start | bytes 2097152 | tf_op jit(solution)/shard_map/all_to_all | solution.py:277
  141.2 29.5 %all-to-all-start.1 = ((bf16[32,4,16,256]{3,2,1,0:T(8,128)(2,1)}), bf16[32,4,16,256]{3,2,1,0:T(8,128)(2,1)S(1)}, u32[]{:S(2)}, u32[]{:S(2)}) async-start(bf16[32,4,16,256]{3,2,1,0:T(8,128)(2,1)} %grid_section.2), calls=%async_computation.1 | async-start | bytes 2097152 | tf_op jit(solution)/shard_map/all_to_all | solution.py:277
